TPU v7x, 32 devices: a whole 2x2x4 slice. The times are simulated.
32 devices in a mesh: ent: 16 (over z, y, x), rep: 2 (over core).
Axes of the slice: x: 2, y: 2, z: 4, core: 2. Of those that a mesh axis runs over, the one named last changes fastest.
Arguments:
- head_ids: int32 [8192], P(('ent', 'rep')), may hold values from 0 to 32767, as said below
- rel_ids: int32 [8192], P(('ent', 'rep')), may hold values from 0 to 4095
- tail_ids: int32 [8192], P(('ent', 'rep')), may hold values from 0 to 32767, as said below
- neg_ids: int32 [256], P('ent'), may hold values from 0 to 32767, as said below
- slot_of: int32 [32768], replicated, may hold values from 0 to 32767, as said below
- relations: bfloat16 [4096, 400], replicated, may hold values from -3 to 3
- embeddings: float32 [32768, 400], P('ent'), may hold values from -1.75 to 1.75
- accumulator: float32 [32768], P('ent'), may hold values from 0.001 to 0.03
Outputs:
- new_embeddings: float32 [32768, 400], P('ent')
- new_accumulator: float32 [32768], P('ent')
Inputs may be any that keep to these rules, and one draw needn't show every extreme that they name: A permutation: every table row stores exactly one entity; the owner of entity e is slot_of[e] // 2048. `head_ids`: among the 512 endpoints (heads and tails together) of the edges of one device, at most 64 have any one owner; in every draw one owner has exactly 64 endpoints of every device. `tail_ids`: see head_ids: the bound counts heads and tails of one device together. `neg_ids`: entry j has owner j // 16.
All inputs are finite; a program needn't handle non-finite values.
Results may differ from a plain program's by a relative error of at most 0.0031.
Values may be sent and summed in bfloat16 or wider, within the bound.
No kernel may reach another device: no remote copies, remote signals or barrier semaphores. Data moves between devices by JAX's collectives and lax.ppermute only.
A program may use at most 128 MiB of HBM per device.

v0:
```python
import jax
import jax.numpy as jnp
from jax import lax
from jax.sharding import PartitionSpec as P

step_rate = 0.3


def split_parts(values):
    cut = values.shape[1] // 2
    return (values[:, :cut], values[:, cut:])


def edge_terms(head_rows, rel_rows, tail_rows, neg_rows):
    head_full = head_rows.astype(jnp.float32)
    rel_full = rel_rows.astype(jnp.float32)
    tail_full = tail_rows.astype(jnp.float32)
    head_re, head_im = split_parts(head_full)
    rel_re, rel_im = split_parts(rel_full)
    tail_re, tail_im = split_parts(tail_full)
    product = jnp.concatenate(
        [head_re * rel_re - head_im * rel_im, head_re * rel_im + head_im * rel_re], axis=1
    )
    product_low = product.astype(jnp.bfloat16)
    mirror_low = jnp.concatenate(
        [rel_re * tail_re + rel_im * tail_im, rel_re * tail_im - rel_im * tail_re], axis=1
    ).astype(jnp.bfloat16)
    positive = jnp.sum(product * tail_full, axis=1)
    inner_dims = (((1,), (1,)), ((), ()))
    tail_scores = lax.dot_general(
        product_low, neg_rows, inner_dims, preferred_element_type=jnp.float32
    )
    head_scores = lax.dot_general(
        mirror_low, neg_rows, inner_dims, preferred_element_type=jnp.float32
    )
    neg_count = neg_rows.shape[0]
    pos_grad = -jax.nn.sigmoid(-positive)
    tail_weight = (jax.nn.sigmoid(tail_scores) / neg_count).astype(jnp.bfloat16)
    head_weight = (jax.nn.sigmoid(head_scores) / neg_count).astype(jnp.bfloat16)
    product_grad = (
        jnp.dot(tail_weight, neg_rows, preferred_element_type=jnp.float32)
        + pos_grad[:, None] * tail_full
    )
    mirror_grad = jnp.dot(head_weight, neg_rows, preferred_element_type=jnp.float32)
    edge_dims = (((0,), (0,)), ((), ()))
    neg_grad = lax.dot_general(
        tail_weight, product_low, edge_dims, preferred_element_type=jnp.float32
    )
    neg_grad = neg_grad + lax.dot_general(
        head_weight, mirror_low, edge_dims, preferred_element_type=jnp.float32
    )
    grad_re, grad_im = split_parts(product_grad)
    head_grad = jnp.concatenate(
        [grad_re * rel_re + grad_im * rel_im, grad_im * rel_re - grad_re * rel_im], axis=1
    )
    back_re, back_im = split_parts(mirror_grad)
    tail_grad = pos_grad[:, None] * product + jnp.concatenate(
        [back_re * rel_re - back_im * rel_im, back_re * rel_im + back_im * rel_re], axis=1
    )
    return (head_grad, tail_grad, neg_grad)


def row_update(old_rows, old_state, gradient):
    new_state = old_state + jnp.mean(gradient * gradient, axis=1)
    new_rows = old_rows - step_rate * gradient / jnp.sqrt(new_state)[:, None]
    return (new_rows, new_state)


def shards(head_ids, rel_ids, tail_ids, neg_ids, slot_of, relations, embeddings, accumulator):
    row_count = embeddings.shape[0]
    feature_count = embeddings.shape[1]
    owner_count = lax.axis_size("ent")
    edge_count = head_ids.shape[0]
    end_ids = jnp.concatenate([head_ids, tail_ids])
    end_count = end_ids.shape[0]
    capacity = 2 * end_count // owner_count
    end_slots = slot_of[end_ids]
    owner_of = end_slots // row_count
    local_row = end_slots % row_count
    sorter = jnp.argsort(owner_of, stable=True)
    sorted_owner = owner_of[sorter]
    per_owner = jnp.sum(
        (owner_of[:, None] == jnp.arange(owner_count, dtype=jnp.int32)[None, :]).astype(jnp.int32),
        axis=0,
    )
    starting = jnp.cumsum(per_owner) - per_owner
    sorted_place = (
        sorted_owner * capacity + jnp.arange(end_count, dtype=jnp.int32) - starting[sorted_owner]
    )
    placed = jnp.zeros((end_count,), jnp.int32).at[sorter].set(sorted_place)
    requests = (
        jnp.full((owner_count * capacity,), -1, jnp.int32)
        .at[placed]
        .set(local_row)
        .reshape(owner_count, capacity)
    )
    low_table = embeddings.astype(jnp.bfloat16)
    asked_rows = lax.all_to_all(requests, "ent", split_axis=0, concat_axis=0, tiled=True)
    picked = jnp.where(
        (asked_rows >= 0)[:, :, None],
        low_table[jnp.maximum(asked_rows, 0)],
        jnp.zeros((), jnp.bfloat16),
    )
    returned = lax.all_to_all(picked, "ent", split_axis=0, concat_axis=0, tiled=True)
    fetched, asked_rows = (returned, asked_rows)
    end_rows = fetched.reshape(owner_count * capacity, feature_count)[placed]
    neg_local = slot_of[neg_ids] % row_count
    own_negs = low_table[neg_local]
    neg_rows = lax.all_gather(own_negs, "ent", axis=0, tiled=True)
    rel_rows = relations[rel_ids]
    head_grad, tail_grad, neg_grad = edge_terms(
        end_rows[:edge_count], rel_rows, end_rows[edge_count:], neg_rows
    )
    neg_part = lax.psum_scatter(neg_grad, "ent", scatter_dimension=0, tiled=True)
    outgoing = (
        jnp.zeros((owner_count * capacity, feature_count), jnp.float32)
        .at[placed]
        .set(jnp.concatenate([head_grad, tail_grad], axis=0))
    )
    incoming = lax.all_to_all(
        outgoing.reshape(owner_count, capacity, feature_count),
        "ent",
        split_axis=0,
        concat_axis=0,
        tiled=True,
    ).reshape(-1, feature_count)
    targets = jnp.where(asked_rows >= 0, asked_rows, row_count).reshape(-1)
    partial_sum = jax.ops.segment_sum(incoming, targets, num_segments=row_count + 1)[:row_count]
    partial_sum = partial_sum.at[neg_local].add(neg_part)
    summed = lax.psum(partial_sum, "rep")
    new_rows, new_state = row_update(embeddings, accumulator, summed)
    return (new_rows, new_state)


def solution(mesh):
    placed = (
        P(("ent", "rep")),
        P(("ent", "rep")),
        P(("ent", "rep")),
        P("ent"),
        P(),
        P(),
        P("ent", None),
        P("ent"),
    )
    return jax.shard_map(
        shards, mesh=mesh, in_specs=placed, out_specs=(P("ent", None), P("ent")), check_vma=False
    )
```

profile of v0, /device:TPU:0, one launch (start us, length us, event | category | flops | bytes accessed | tf_op | source)
XLA Modules:
  0.0 261.9 jit_solution(16662489668703026024)
XLA Ops:
  8.1 3.1 %gather_fusion = s32[512]{0:T(512)S(1)} fusion(s32[32768]{0:T(1024)S(1)} %copy-done, s32[1024]{0:T(1024)S(1)} %pad_clamp_fusion.5), kind=kCustom, calls=%fused_computation | custom fusion | bytes 6144 | tf_op jit(solution)/shard_map/gather | solution.py:77
  11.4 3.8 %sort.17 = (s32[512]{0:T(512)}, s32[512]{0:T(512)S(1)}) sort(s32[512]{0:T(512)S(1)} %get-tuple-element.38, s32[512]{0:T(512)S(1)} %iota.11), dimensions={0}, to_apply=%region_0.1 | sort | flops 4608 | bytes 8192 | tf_op jit(solution)/shard_map/jit(argsort)/sort | solution.py:80
  15.1 3.5 %gather_fusion.1 = s32[512]{0:T(512)S(1)} fusion(s32[512]{0:T(512)S(1)} %get-tuple-element.38, s32[1024]{0:T(1024)S(1)} %pad_clamp_fusion.4), kind=kCustom, calls=%fused_computation.1 | custom fusion | bytes 6144 | tf_op jit(solution)/shard_map/gather | solution.py:81
  19.6 4.4 %compare_select_fusion.3 = (s32[512,1]{0,1:T(1,128)S(1)}, s32[512,1]{0,1:T(1,128)S(1)}) fusion(s32[]{:T(128)} %bitcast.14, s32[]{:T(128)} %bitcast.15, s32[]{:T(128)} %bitcast.16, s32[]{:T(128)} %bitcast.17, s32[]{:T(128)} %bitcast.18, s32[]{:T(128)} %bitcast.20, s32[]{:T(128)} %bitcast.19, s32[512,1]{0,1:T(1,128)S(1)} %bitcast.53), kind=kLoop, calls=%fused_computation.63 | loop fusion | flops 7680 | bytes 6172 | tf_op jit(solution)/shard_map/gather | solution.py:88
  24.0 5.7 %select_subtract_fusion = s32[512]{0:T(512)S(1)} fusion(pred[512]{0:T(512)(128)(4,1)S(1)} %get-tuple-element.20, pred[512]{0:T(512)(128)(4,1)S(1)} %get-tuple-element.19, pred[512]{0:T(512)(128)(4,1)S(1)} %get-tuple-element.18, pred[512]{0:T(512)(128)(4,1)S(1)} %get-tuple-element.17, pred[512]{0:T(512)(128)(4,1)S(1)} %get-tuple-element.16, ...), kind=kLoop, calls=%fused_computation.90 | loop fusion | flops 6144 | bytes 10788 | tf_op jit(solution)/shard_map/sub | solution.py:88
  35.3 8.3 %all-to-all-start = ((s32[16,1,64]{2,1,0:T(1,128)}), s32[16,1,64]{2,1,0:T(1,128)S(1)}, u32[]{:S(2)}, u32[]{:S(2)}) async-start(s32[16,1,64]{2,1,0:T(1,128)} %all_to_all.14), calls=%async_computation | async-start | bytes 16384 | tf_op jit(solution)/shard_map/all_to_all | solution.py:98
  43.7 3.4 %copy.54 = f32[2048,400]{1,0:T(8,128)} copy(f32[2048,400]{0,1:T(8,128)S(1)} %copy-done.2) | data formatting | bytes 6553600 | tf_op args[6]
  47.0 2.5 convert_element_type.26
  51.0 4.0 %gather_fusion.2 = bf16[1024,400]{1,0:T(8,128)(2,1)S(1)} fusion(bf16[2048,400]{1,0:T(8,128)(2,1)S(1)} %convert_element_type.26, s32[1024]{0:T(1024)S(1)} %broadcast_clamp_fusion), kind=kCustom, calls=%fused_computation.2 | custom fusion | bytes 1642496 | tf_op jit(solution)/shard_map/gather | solution.py:101
  56.1 5.5 %all-to-all-start.1 = ((bf16[16,64,400]{2,1,0:T(8,128)(2,1)}), bf16[16,64,400]{2,1,0:T(8,128)(2,1)S(1)}, u32[]{:S(2)}, u32[]{:S(2)}) async-start(bf16[16,64,400]{2,1,0:T(8,128)(2,1)} %broadcast_select_fusion), calls=%async_computation.1 | async-start | bytes 2097152 | tf_op jit(solution)/shard_map/all_to_all | solution.py:104
  63.0 6.0 %copy.50 = bf16[4096,400]{1,0:T(8,128)(2,1)} copy(bf16[4096,400]{0,1:T(8,128)(2,1)} %param.13) | data formatting | bytes 6553600 | tf_op args[5]
  69.0 3.9 %gather_fusion.4 = bf16[256,400]{1,0:T(8,128)(2,1)S(1)} fusion(bf16[4096,400]{1,0:T(8,128)(2,1)} %copy.50, s32[1024]{0:T(1024)S(1)} %pad_clamp_fusion.2), kind=kCustom, calls=%fused_computation.4 | custom fusion | bytes 410624 | tf_op jit(solution)/shard_map/gather | solution.py:110
  73.1 42.7 %all-gather = bf16[256,400]{1,0:T(8,128)(2,1)S(1)} all-gather(bf16[16,400]{1,0:T(8,128)(2,1)S(1)} %gather_fusion.6), channel_id=2, replica_groups=mesh['ent'=16,'rep'=2] {'ent'}, dimensions={0}, use_global_device_ids=true | all-gather | bytes 217600 | tf_op jit(solution)/shard_map/all_gather | solution.py:109
  121.3 3.6 %scatter_custom_fusion.2 = f32[1024,400]{1,0:T(8,128)} fusion(s32[512]{0:T(512)S(1)} %compare_select_fusion.9, f32[512,400]{1,0:T(8,128)S(1)} %copy.53, f32[]{:T(128)} %constant.29.clone.1), kind=kCustom, calls=%fused_computation.30 | custom fusion | bytes 1638404 | tf_op jit(solution)/shard_map/scatter | solution.py:118
  125.0 3.7 %all-to-all-start.2 = ((f32[16,64,400]{2,1,0:T(8,128)}), f32[16,64,400]{2,1,0:T(8,128)S(1)}, u32[]{:S(2)}, u32[]{:S(2)}) async-start(f32[16,64,400]{2,1,0:T(8,128)} %bitcast.30), calls=%async_computation.2 | async-start | bytes 4194304 | tf_op jit(solution)/shard_map/all_to_all | solution.py:120
  131.5 37.4 %all-to-all-done.2 = f32[16,64,400]{2,1,0:T(8,128)S(1)} async-done(((f32[16,64,400]{2,1,0:T(8,128)}), f32[16,64,400]{2,1,0:T(8,128)S(1)}, u32[]{:S(2)}, u32[]{:S(2)}) %all-to-all-start.2) | async-done | bytes 1638432 | tf_op jit(solution)/shard_map/all_to_all | solution.py:120
  168.9 9.2 %scatter_custom_fusion.3 = f32[2049,400]{1,0:T(8,128)} fusion(s32[1024]{0:T(1024)S(1)} %bitcast.56, f32[1024,400]{1,0:T(8,128)S(1)} %bitcast.50, f32[]{:T(128)} %constant.29.clone.1), kind=kCustom, calls=%fused_computation.14 | custom fusion | flops 409600 | bytes 3278404 | tf_op jit(solution)/shard_map/scatter-add | solution.py:128
  178.1 4.6 %slice.95 = f32[2048,400]{1,0:T(8,128)} slice(f32[2049,400]{1,0:T(8,128)} %scatter_custom_fusion.3), slice={[0:2048], [0:400]} | slice | bytes 6553600 | tf_op jit(solution)/shard_map/slice | solution.py:128
  182.7 29.2 %reduce-scatter.2.cloned.1.call-done = f32[16,400]{1,0:T(8,128)} async-done(((f32[256,400]{1,0:T(8,128)}), f32[16,400]{1,0:T(8,128)}) %reduce-scatter.2.cloned.1.call-update) | async-done | bytes 25616 | tf_op jit(solution)/shard_map/reduce_scatter | solution.py:114
  211.9 5.0 %scatter_fusion = f32[2048,400]{1,0:T(8,128)} fusion(f32[2048,400]{1,0:T(8,128)} %slice.95, s32[16]{0:T(128)S(1)} %fusion.24, f32[16,400]{1,0:T(8,128)} %reduce-scatter.2.cloned.1.call-done), kind=kCustom, calls=%fused_computation.11 | custom fusion | flops 6400 | bytes 76864 | tf_op jit(solution)/shard_map/scatter-add | solution.py:129
  217.0 24.6 %all-reduce.2.cloned.1.call-done = f32[2048,400]{1,0:T(8,128)} async-done(((f32[2048,400]{1,0:T(8,128)}), f32[2048,400]{1,0:T(8,128)}) %all-reduce.2.cloned.1.call-update) | async-done | bytes 3276816 | tf_op jit(solution)/shard_map/psum | solution.py:130
  241.6 2.7 %multiply_reduce_fusion = f32[2048]{0:T(1024)S(1)} fusion(f32[2048,400]{1,0:T(8,128)} %all-reduce.2.cloned.1.call-done), kind=kLoop, calls=%fused_computation.13 | loop fusion | flops 1636352 | bytes 3284992 | tf_op jit(solution)/shard_map/reduce_sum | solution.py:64
  245.0 4.9 %divide_subtract_fusion = f32[2048,400]{1,0:T(8,128)} fusion(f32[2048,400]{1,0:T(8,128)S(1)} %copy-done.1, f32[2048,400]{1,0:T(8,128)} %all-reduce.2.cloned.1.call-done, f32[2048]{0:T(1024)S(1)} %get-tuple-element.21), kind=kLoop, calls=%fused_computation.12 | loop fusion | flops 2457600 | bytes 9838592 | tf_op jit(solution)/shard_map/sub | solution.py:65
  249.9 5.2 %copy.55 = f32[2048,400]{0,1:T(8,128)} copy(f32[2048,400]{1,0:T(8,128)} %divide_subtract_fusion) | data formatting | bytes 6553600
  (92 shorter events, 20.5 us)
Async XLA Ops:
  7.2 0.9 copy-start
  7.2 36.5 %copy-start.2 = (f32[2048,400]{0,1:T(8,128)S(1)}, f32[2048,400]{0,1:T(8,128)}, u32[]{:S(2)}) copy-start(f32[2048,400]{0,1:T(8,128)} %param.14) | copy-start | bytes 9830404
  35.3 15.6 %all-to-all-start = ((s32[16,1,64]{2,1,0:T(1,128)}), s32[16,1,64]{2,1,0:T(1,128)S(1)}, u32[]{:S(2)}, u32[]{:S(2)}) async-start(s32[16,1,64]{2,1,0:T(1,128)} %all_to_all.14), calls=%async_computation | async-start | bytes 16384 | tf_op jit(solution)/shard_map/all_to_all | solution.py:98
  54.9 6.7 %copy-start.13 = (s32[16]{0:T(128)S(1)}, s32[16]{0:T(128)}, u32[]{:S(2)}) copy-start(s32[16]{0:T(128)} %param.11) | copy-start | bytes 196
  56.1 59.8 %all-to-all-start.1 = ((bf16[16,64,400]{2,1,0:T(8,128)(2,1)}), bf16[16,64,400]{2,1,0:T(8,128)(2,1)S(1)}, u32[]{:S(2)}, u32[]{:S(2)}) async-start(bf16[16,64,400]{2,1,0:T(8,128)(2,1)} %broadcast_select_fusion), calls=%async_computation.1 | async-start | bytes 2097152 | tf_op jit(solution)/shard_map/all_to_all | solution.py:104
  61.7 7.3 %copy-start.12 = (s32[256]{0:T(256)S(1)}, s32[256]{0:T(256)}, u32[]{:S(2)}) copy-start(s32[256]{0:T(256)} %param.9) | copy-start | bytes 3076
  118.8 0.6 copy-start.3
  119.1 0.6 copy-start.7
  119.2 0.7 copy-start.9
  120.1 0.7 copy-start.5
  121.3 7.5 %copy-start.4 = (bf16[256,256]{1,0:T(8,128)(2,1)S(1)}, bf16[256,256]{1,0:T(8,128)(2,1)}, u32[]{:S(2)}) copy-start(bf16[256,256]{1,0:T(8,128)(2,1)} %copy-done.3) | copy-start | bytes 393220
  121.3 7.7 %copy-start.6 = (bf16[256,256]{1,0:T(8,128)(2,1)S(1)}, bf16[256,256]{1,0:T(8,128)(2,1)}, u32[]{:S(2)}) copy-start(bf16[256,256]{1,0:T(8,128)(2,1)} %copy-done.5) | copy-start | bytes 393220
  121.3 7.7 %copy-start.8 = (bf16[256,200]{0,1:T(8,128)(2,1)S(1)}, bf16[256,200]{0,1:T(8,128)(2,1)}, u32[]{:S(2)}) copy-start(bf16[256,200]{0,1:T(8,128)(2,1)} %copy-done.7) | copy-start | bytes 307204
  121.3 7.7 %copy-start.10 = (bf16[256,200]{0,1:T(8,128)(2,1)S(1)}, bf16[256,200]{0,1:T(8,128)(2,1)}, u32[]{:S(2)}) copy-start(bf16[256,200]{0,1:T(8,128)(2,1)} %copy-done.9) | copy-start | bytes 307204
  125.0 44.0 %all-to-all-start.2 = ((f32[16,64,400]{2,1,0:T(8,128)}), f32[16,64,400]{2,1,0:T(8,128)S(1)}, u32[]{:S(2)}, u32[]{:S(2)}) async-start(f32[16,64,400]{2,1,0:T(8,128)} %bitcast.30), calls=%async_computation.2 | async-start | bytes 4194304 | tf_op jit(solution)/shard_map/all_to_all | solution.py:120
  128.7 83.2 %reduce-scatter.2.cloned.1.call-start = ((), (), s32[]{:S(2)}) async-start(), calls=%async_computation.4 | async-start | bytes 557056 | tf_op jit(solution)/shard_map/reduce_scatter | solution.py:114
  130.2 111.3 %all-reduce.2.cloned.1.call-start = ((), (), s32[]{:S(2)}) async-start(), calls=%async_computation.5 | async-start | bytes 8388608 | tf_op jit(solution)/shard_map/psum | solution.py:130
  217.0 27.3 %copy-start.11 = (f32[2048]{0:T(1024)S(1)}, f32[2048]{0:T(1024)}, u32[]{:S(2)}) copy-start(f32[2048]{0:T(1024)} %param.15) | copy-start | bytes 24580
  241.6 3.4 %copy-start.1 = (f32[2048,400]{1,0:T(8,128)S(1)}, f32[2048,400]{1,0:T(8,128)}, u32[]{:S(2)}) copy-start(f32[2048,400]{1,0:T(8,128)} %copy.54) | copy-start | bytes 9830404
Sparse Core Ops, SparseCore 0:
  131.8 80.1 reduce-scatter.1
  217.1 24.4 all-reduce.1
where the time goes:
time: 263 us; the launch traced here: 262 us
  waiting for transfers between devices  92.6 us (35%)
  local copies, waits for them, and re-layouts  49.5 us (19%)
  blocking collectives  42.7 us (16%)
  other arithmetic  42.3 us (16%)
  starting transfers between devices  17.7 us (7%)
  between operations  14.5 us (6%)
    all_gather x1, blocking collectives, shards(): neg_rows = lax.all_gather(own_negs, 'ent', axis=0, tiled=True)  42.7 us
    all_to_all x1, waiting for transfers between devices, shards(): lax.all_to_all(outgoing.reshape(owner_count, capacity, feature_count), 'e...  37.4 us
    reduce_scatter x1, waiting for transfers between devices, shards(): lax.psum_scatter(neg_grad, 'ent', scatter_dimension=0, tiled=True)  29.2 us
    psum x1, waiting for transfers between devices, shards(): summed = lax.psum(partial_sum, 'rep')  24.6 us
    unnamed x33, local copies, waits for them, and re-layouts  16 us
    scatter-add x1, other arithmetic, shards(): jax.ops.segment_sum(incoming, targets, num_segments=row_count + 1)  9.16 us
    all_to_all x1, starting transfers between devices, shards(): lax.all_to_all(requests, 'ent', split_axis=0, concat_axis=0, tiled=True)  8.34 us
    sub x1, other arithmetic, shards(): sorted_owner * capacity + jnp.arange(end_count, dtype=jnp.int32)  5.67 us
  transfers between devices with their start and end apart: 5, of which 4 were waited for; matrix products, arithmetic and copies ran while one was open for 13% of the time, Pallas kernels for 0%

commit v1 on v0

--- a/solution.py
+++ b/solution.py
@@ -127,7 +127,8 @@
     targets = jnp.where(asked_rows >= 0, asked_rows, row_count).reshape(-1)
     partial_sum = jax.ops.segment_sum(incoming, targets, num_segments=row_count + 1)[:row_count]
     partial_sum = partial_sum.at[neg_local].add(neg_part)
-    summed = lax.psum(partial_sum, "rep")
+    blocks = lax.all_gather(partial_sum, "rep")
+    summed = jnp.sum(blocks, axis=0)
     new_rows, new_state = row_update(embeddings, accumulator, summed)
     return (new_rows, new_state)
 

time: 263 us -> 282 us (1.072)
  other arithmetic: 42.3 us -> 61 us
  local copies, waits for them, and re-layouts: 49.5 us -> 59.7 us
  waiting for transfers between devices: 92.6 us -> 84.2 us
    reduce_sum x0 -> x1, other arithmetic: none -> 26.1 us  [shards(): summed = jnp.sum(blocks, axis=0)]
    psum x1 -> x0, waiting for transfers between devices: 24.6 us -> none  [shards(): summed = lax.psum(partial_sum, 'rep')]
    all_gather x0 -> x1, waiting for transfers between devices: none -> 13.6 us  [shards(): blocks = lax.all_gather(partial_sum, 'rep')]
    all_gather x0 -> x1, local copies, waits for them, and re-layouts: none -> 9.39 us  [shards(): blocks = lax.all_gather(partial_sum, 'rep')]
    scatter-add x0 -> x1, local copies, waits for them, and re-layouts: none -> 5.17 us  [shards(): partial_sum = partial_sum.at[neg_local].add(neg_part)]
    unnamed x33 -> x30, local copies, waits for them, and re-layouts: 16 us -> 11.7 us
  transfers between devices with their start and end apart: 5 -> 5, of which waited for: 4 -> 4; matrix products, arithmetic and copies ran while one was open for 13% -> 11% of each run, Pallas kernels for 0% -> 0%
where the time goes in v1:
time: 282 us; the launch traced here: 281 us
  waiting for transfers between devices  84.2 us (30%)
  other arithmetic  61 us (22%)
  local copies, waits for them, and re-layouts  59.7 us (21%)
  blocking collectives  42.7 us (15%)
  starting transfers between devices  16 us (6%)
  between operations  14.5 us (5%)
    all_gather x1, blocking collectives, shards(): neg_rows = lax.all_gather(own_negs, 'ent', axis=0, tiled=True)  42.7 us
    all_to_all x1, waiting for transfers between devices, shards(): lax.all_to_all(outgoing.reshape(owner_count, capacity, feature_count), 'e...  37 us
    reduce_scatter x1, waiting for transfers between devices, shards(): lax.psum_scatter(neg_grad, 'ent', scatter_dimension=0, tiled=True)  29.5 us
    reduce_sum x1, other arithmetic, shards(): summed = jnp.sum(blocks, axis=0)  26.1 us
    all_gather x1, waiting for transfers between devices, shards(): blocks = lax.all_gather(partial_sum, 'rep')  13.6 us
    unnamed x30, local copies, waits for them, and re-layouts  11.7 us
    all_gather x1, local copies, waits for them, and re-layouts, shards(): blocks = lax.all_gather(partial_sum, 'rep')  9.39 us
    scatter-add x1, other arithmetic, shards(): jax.ops.segment_sum(incoming, targets, num_segments=row_count + 1)  9.16 us
  transfers between devices with their start and end apart: 5, of which 4 were waited for; matrix products, arithmetic and copies ran while one was open for 11% of the time, Pallas kernels for 0%

profile of v1, /device:TPU:0, one launch (start us, length us, event | category | flops | bytes accessed | tf_op | source)
XLA Modules:
  0.0 280.6 jit_solution(16003686654528126458)
XLA Ops:
  8.1 3.1 %gather_fusion = s32[512]{0:T(512)S(1)} fusion(s32[32768]{0:T(1024)S(1)} %copy-done, s32[1024]{0:T(1024)S(1)} %pad_clamp_fusion.5), kind=kCustom, calls=%fused_computation | custom fusion | bytes 6144 | tf_op jit(solution)/shard_map/gather | solution.py:77
  11.4 3.8 %sort.17 = (s32[512]{0:T(512)}, s32[512]{0:T(512)S(1)}) sort(s32[512]{0:T(512)S(1)} %get-tuple-element.30, s32[512]{0:T(512)S(1)} %iota.11), dimensions={0}, to_apply=%region_0.1 | sort | flops 4608 | bytes 8192 | tf_op jit(solution)/shard_map/jit(argsort)/sort | solution.py:80
  15.2 3.5 %gather_fusion.1 = s32[512]{0:T(512)S(1)} fusion(s32[512]{0:T(512)S(1)} %get-tuple-element.30, s32[1024]{0:T(1024)S(1)} %pad_clamp_fusion.4), kind=kCustom, calls=%fused_computation.1 | custom fusion | bytes 6144 | tf_op jit(solution)/shard_map/gather | solution.py:81
  19.6 4.4 %compare_select_fusion.3 = (s32[512,1]{0,1:T(1,128)S(1)}, s32[512,1]{0,1:T(1,128)S(1)}) fusion(s32[]{:T(128)} %bitcast.14, s32[]{:T(128)} %bitcast.15, s32[]{:T(128)} %bitcast.16, s32[]{:T(128)} %bitcast.17, s32[]{:T(128)} %bitcast.18, s32[]{:T(128)} %bitcast.20, s32[]{:T(128)} %bitcast.19, s32[512,1]{0,1:T(1,128)S(1)} %bitcast.55), kind=kLoop, calls=%fused_computation.63 | loop fusion | flops 7680 | bytes 6172 | tf_op jit(solution)/shard_map/gather | solution.py:88
  24.1 5.7 %select_subtract_fusion = s32[512]{0:T(512)S(1)} fusion(pred[512]{0:T(512)(128)(4,1)S(1)} %get-tuple-element.12, pred[512]{0:T(512)(128)(4,1)S(1)} %get-tuple-element.11, pred[512]{0:T(512)(128)(4,1)S(1)} %get-tuple-element.10, pred[512]{0:T(512)(128)(4,1)S(1)} %get-tuple-element.9, pred[512]{0:T(512)(128)(4,1)S(1)} %get-tuple-element.8, ...), kind=kLoop, calls=%fused_computation.90 | loop fusion | flops 6144 | bytes 10788 | tf_op jit(solution)/shard_map/sub | solution.py:88
  35.3 8.3 %all-to-all-start = ((s32[16,1,64]{2,1,0:T(1,128)}), s32[16,1,64]{2,1,0:T(1,128)S(1)}, u32[]{:S(2)}, u32[]{:S(2)}) async-start(s32[16,1,64]{2,1,0:T(1,128)} %all_to_all.14), calls=%async_computation | async-start | bytes 16384 | tf_op jit(solution)/shard_map/all_to_all | solution.py:98
  43.7 3.1 %copy.52 = bf16[2048,400]{1,0:T(8,128)(2,1)S(1)} copy(f32[2048,400]{0,1:T(8,128)} %param.14) | data formatting | bytes 4915200 | tf_op args[6]
  46.8 4.1 %all-to-all-done = s32[16,1,64]{2,1,0:T(1,128)S(1)} async-done(((s32[16,1,64]{2,1,0:T(1,128)}), s32[16,1,64]{2,1,0:T(1,128)S(1)}, u32[]{:S(2)}, u32[]{:S(2)}) %all-to-all-start) | async-done | bytes 4128 | tf_op jit(solution)/shard_map/all_to_all | solution.py:98
  51.0 4.0 %gather_fusion.2 = bf16[1024,400]{1,0:T(8,128)(2,1)S(1)} fusion(bf16[2048,400]{1,0:T(8,128)(2,1)S(1)} %copy.52, s32[1024]{0:T(1024)S(1)} %broadcast_clamp_fusion), kind=kCustom, calls=%fused_computation.2 | custom fusion | bytes 1642496 | tf_op jit(solution)/shard_map/gather | solution.py:101
  56.2 3.7 %all-to-all-start.1 = ((bf16[16,64,400]{2,1,0:T(8,128)(2,1)}), bf16[16,64,400]{2,1,0:T(8,128)(2,1)S(1)}, u32[]{:S(2)}, u32[]{:S(2)}) async-start(bf16[16,64,400]{2,1,0:T(8,128)(2,1)} %broadcast_select_fusion), calls=%async_computation.1 | async-start | bytes 2097152 | tf_op jit(solution)/shard_map/all_to_all | solution.py:104
  61.1 6.0 %copy.55 = bf16[4096,400]{1,0:T(8,128)(2,1)} copy(bf16[4096,400]{0,1:T(8,128)(2,1)} %param.13) | data formatting | bytes 6553600 | tf_op args[5]
  67.2 3.9 %gather_fusion.4 = bf16[256,400]{1,0:T(8,128)(2,1)S(1)} fusion(bf16[4096,400]{1,0:T(8,128)(2,1)} %copy.55, s32[1024]{0:T(1024)S(1)} %pad_clamp_fusion.2), kind=kCustom, calls=%fused_computation.4 | custom fusion | bytes 410624 | tf_op jit(solution)/shard_map/gather | solution.py:110
  71.3 42.7 %all-gather = bf16[256,400]{1,0:T(8,128)(2,1)S(1)} all-gather(bf16[16,400]{1,0:T(8,128)(2,1)S(1)} %gather_fusion.6), channel_id=2, replica_groups=mesh['ent'=16,'rep'=2] {'ent'}, dimensions={0}, use_global_device_ids=true | all-gather | bytes 217600 | tf_op jit(solution)/shard_map/all_gather | solution.py:109
  119.4 3.6 %scatter_custom_fusion.2 = f32[1024,400]{1,0:T(8,128)} fusion(s32[512]{0:T(512)S(1)} %compare_select_fusion.9, f32[512,400]{1,0:T(8,128)S(1)} %copy.58, f32[]{:T(128)} %constant.29.clone.1), kind=kCustom, calls=%fused_computation.30 | custom fusion | bytes 1638404 | tf_op jit(solution)/shard_map/scatter | solution.py:118
  123.1 3.9 %all-to-all-start.2 = ((f32[16,64,400]{2,1,0:T(8,128)}), f32[16,64,400]{2,1,0:T(8,128)S(1)}, u32[]{:S(2)}, u32[]{:S(2)}) async-start(f32[16,64,400]{2,1,0:T(8,128)} %bitcast.30), calls=%async_computation.2 | async-start | bytes 4194304 | tf_op jit(solution)/shard_map/all_to_all | solution.py:120
  129.8 37.0 %all-to-all-done.2 = f32[16,64,400]{2,1,0:T(8,128)S(1)} async-done(((f32[16,64,400]{2,1,0:T(8,128)}), f32[16,64,400]{2,1,0:T(8,128)S(1)}, u32[]{:S(2)}, u32[]{:S(2)}) %all-to-all-start.2) | async-done | bytes 1638432 | tf_op jit(solution)/shard_map/all_to_all | solution.py:120
  166.9 9.2 %scatter_custom_fusion.3 = f32[2049,400]{1,0:T(8,128)} fusion(s32[1024]{0:T(1024)S(1)} %bitcast.58, f32[1024,400]{1,0:T(8,128)S(1)} %bitcast.52, f32[]{:T(128)} %constant.29.clone.1), kind=kCustom, calls=%fused_computation.14 | custom fusion | flops 409600 | bytes 3278404 | tf_op jit(solution)/shard_map/scatter-add | solution.py:128
  176.0 4.6 %slice.95 = f32[2048,400]{1,0:T(8,128)} slice(f32[2049,400]{1,0:T(8,128)} %scatter_custom_fusion.3), slice={[0:2048], [0:400]} | slice | bytes 6553600 | tf_op jit(solution)/shard_map/slice | solution.py:128
  180.6 29.5 %reduce-scatter.2.cloned.1.call-done = f32[16,400]{1,0:T(8,128)} async-done(((f32[256,400]{1,0:T(8,128)}), f32[16,400]{1,0:T(8,128)}) %reduce-scatter.2.cloned.1.call-update) | async-done | bytes 25616 | tf_op jit(solution)/shard_map/reduce_scatter | solution.py:114
  210.1 5.0 %scatter_fusion = f32[2048,400]{1,0:T(8,128)} fusion(f32[2048,400]{1,0:T(8,128)} %slice.95, s32[16]{0:T(128)S(1)} %fusion.24, f32[16,400]{1,0:T(8,128)} %reduce-scatter.2.cloned.1.call-done), kind=kCustom, calls=%fused_computation.11 | custom fusion | flops 6400 | bytes 76864 | tf_op jit(solution)/shard_map/scatter-add | solution.py:129
  215.1 5.2 %copy.59 = f32[2048,400]{0,1:T(8,128)} copy(f32[2048,400]{1,0:T(8,128)} %scatter_fusion) | data formatting | bytes 6553600 | tf_op jit(solution)/shard_map/scatter-add | solution.py:129
  220.3 13.6 %all-gather.4.cloned.1.call-done = f32[4096,400]{0,1:T(8,128)} async-done(((f32[2048,400]{0,1:T(8,128)}), f32[4096,400]{0,1:T(8,128)}) %all-gather.4.cloned.1.call-update) | async-done | bytes 6553616 | tf_op jit(solution)/shard_map/all_gather | solution.py:130
  233.9 9.4 %reshape.372 = f32[2,2048,400]{1,0,2:T(2,128)} reshape(f32[4096,400]{0,1:T(8,128)} %all-gather.4.cloned.1.call-done) | data formatting | bytes 13107200 | tf_op jit(solution)/shard_map/all_gather | solution.py:130
  243.3 26.1 %reduce_sum.38 = f32[2048,400]{0,1:T(8,128)S(1)} reduce(f32[2,2048,400]{1,0,2:T(2,128)} %reshape.372, f32[]{:T(128)} %constant.29.clone.1), dimensions={0}, to_apply=%region_10.11 | reduce | flops 819200 | bytes 9830404 | tf_op jit(solution)/shard_map/reduce_sum | solution.py:131
  (91 shorter events, 22.8 us)
Async XLA Ops:
  7.2 0.9 copy-start
  35.3 15.6 %all-to-all-start = ((s32[16,1,64]{2,1,0:T(1,128)}), s32[16,1,64]{2,1,0:T(1,128)S(1)}, u32[]{:S(2)}, u32[]{:S(2)}) async-start(s32[16,1,64]{2,1,0:T(1,128)} %all_to_all.14), calls=%async_computation | async-start | bytes 16384 | tf_op jit(solution)/shard_map/all_to_all | solution.py:98
  55.0 4.9 %copy-start.12 = (s32[16]{0:T(128)S(1)}, s32[16]{0:T(128)}, u32[]{:S(2)}) copy-start(s32[16]{0:T(128)} %param.11) | copy-start | bytes 196
  56.2 57.8 %all-to-all-start.1 = ((bf16[16,64,400]{2,1,0:T(8,128)(2,1)}), bf16[16,64,400]{2,1,0:T(8,128)(2,1)S(1)}, u32[]{:S(2)}, u32[]{:S(2)}) async-start(bf16[16,64,400]{2,1,0:T(8,128)(2,1)} %broadcast_select_fusion), calls=%async_computation.1 | async-start | bytes 2097152 | tf_op jit(solution)/shard_map/all_to_all | solution.py:104
  61.1 6.0 %copy-start.11 = (s32[256]{0:T(256)S(1)}, s32[256]{0:T(256)}, u32[]{:S(2)}) copy-start(s32[256]{0:T(256)} %param.9) | copy-start | bytes 3076
  116.9 0.6 copy-start.2
  117.3 0.6 copy-start.6
  117.3 0.7 copy-start.8
  118.2 0.7 copy-start.4
  119.4 7.6 %copy-start.3 = (bf16[256,256]{1,0:T(8,128)(2,1)S(1)}, bf16[256,256]{1,0:T(8,128)(2,1)}, u32[]{:S(2)}) copy-start(bf16[256,256]{1,0:T(8,128)(2,1)} %copy-done.2) | copy-start | bytes 393220
  119.4 7.9 %copy-start.5 = (bf16[256,256]{1,0:T(8,128)(2,1)S(1)}, bf16[256,256]{1,0:T(8,128)(2,1)}, u32[]{:S(2)}) copy-start(bf16[256,256]{1,0:T(8,128)(2,1)} %copy-done.4) | copy-start | bytes 393220
  119.4 7.9 %copy-start.7 = (bf16[256,200]{0,1:T(8,128)(2,1)S(1)}, bf16[256,200]{0,1:T(8,128)(2,1)}, u32[]{:S(2)}) copy-start(bf16[256,200]{0,1:T(8,128)(2,1)} %copy-done.6) | copy-start | bytes 307204
  119.4 7.9 %copy-start.9 = (bf16[256,200]{0,1:T(8,128)(2,1)S(1)}, bf16[256,200]{0,1:T(8,128)(2,1)}, u32[]{:S(2)}) copy-start(bf16[256,200]{0,1:T(8,128)(2,1)} %copy-done.8) | copy-start | bytes 307204
  123.1 43.8 %all-to-all-start.2 = ((f32[16,64,400]{2,1,0:T(8,128)}), f32[16,64,400]{2,1,0:T(8,128)S(1)}, u32[]{:S(2)}, u32[]{:S(2)}) async-start(f32[16,64,400]{2,1,0:T(8,128)} %bitcast.30), calls=%async_computation.2 | async-start | bytes 4194304 | tf_op jit(solution)/shard_map/all_to_all | solution.py:120
  127.0 83.1 %reduce-scatter.2.cloned.1.call-start = ((), (), s32[]{:S(2)}) async-start(), calls=%async_computation.4 | async-start | bytes 557056 | tf_op jit(solution)/shard_map/reduce_scatter | solution.py:114
  128.5 105.4 %all-gather.4.cloned.1.call-start = ((), (), s32[]{:S(2)}) async-start(), calls=%async_computation.5 | async-start | bytes 9830400 | tf_op jit(solution)/shard_map/all_gather | solution.py:130
  269.4 0.7 copy-start.10
  269.5 1.9 copy-start.1
Sparse Core Ops, SparseCore 0:
  130.1 79.9 reduce-scatter.1
  220.4 13.4 all-gather.3
